TPU v7x, 256 devices: a whole 4x4x8 slice. The times are simulated.
256 devices in a mesh: ctx: 64 (over x_hi, y, z), tp: 4 (over x_lo, core).
Axes of the slice: x: 4 (x_hi: 2, x_lo: 2; x = x_hi * 2 + x_lo), y: 4, z: 8, core: 2. Of those that a mesh axis runs over, the one named last changes fastest.
Arguments:
- hidden: bfloat16 [32768, 5120], P('ctx', 'tp'), may hold values from -6 to 6
- queries: bfloat16 [32768, 5120], P('ctx', 'tp'), may hold values from -600 to 600
- lengths: int32 [256], replicated, may hold values from 1 to 2048, 32768 in all
- norm_gain: float32 [5120], P('tp'), may hold values from 0.5 to 1.5
- kv_weight: bfloat16 [5120, 2, 1024], P(None, None, 'tp'), may hold values from -0.078125 to 0.078125
- kv_bias: float32 [2, 1024], P(None, 'tp'), may hold values from -3 to 3
Outputs:
- attended: bfloat16 [32768, 5120], P('ctx', 'tp')
Inputs may be any that keep to these rules, and one draw needn't show every extreme that they name: The 256 files fill the 32768 positions in order; their lengths sum to 32768 and the longest is exactly 2048.
All inputs are finite; a program needn't handle non-finite values.
Results may differ from a plain program's by a relative error of at most 0.006.
Values may be sent and summed in bfloat16 or wider, within the bound.
A program may use at most 128 MiB of HBM per device.

v0:
```python
import jax
import jax.numpy as jnp
from jax import lax
from jax.sharding import PartitionSpec as P

D = 5120
HD = 128
CYCLE = 4


def shifted(value, axis, steps):
    count = lax.axis_size(axis)
    leading, last = (max(0, -steps), min(count, count - steps))
    return lax.ppermute(value, axis, [(source, source + steps) for source in range(leading, last)])


def body(hidden, queries, lengths, norm_gain, kv_weight, kv_bias):
    tok = hidden.shape[0]
    xfull = hidden.astype(jnp.float32)
    squares = lax.psum(jnp.sum(xfull * xfull, axis=1), "tp")
    scale_rows = lax.rsqrt(squares / D + 1e-06)
    normed = (xfull * scale_rows[:, None] * norm_gain[None, :]).astype(jnp.bfloat16)
    flat_weight = kv_weight.reshape(kv_weight.shape[0], -1)
    summed = jnp.dot(
        lax.all_gather(normed, "tp", axis=1, tiled=True),
        flat_weight,
        preferred_element_type=jnp.float32,
    )
    kv_local = (
        (summed + kv_bias.reshape(-1)[None, :])
        .astype(jnp.bfloat16)
        .reshape(tok, 2, kv_weight.shape[2])
    )
    kv_heads = kv_weight.shape[2] // HD
    group = queries.shape[1] // HD // kv_heads
    qrows = queries.reshape(tok, kv_heads, group, HD)
    device = lax.axis_index("ctx")
    ends = jnp.cumsum(lengths)
    score_scale = HD ** (-0.5)

    def docs_of(first):
        positions = first + jnp.arange(tok, dtype=jnp.int32)
        found = jnp.sum((positions[:, None] >= ends[None, :]).astype(jnp.int32), axis=1)
        return (found, positions)

    qdoc, qpos = docs_of(device * tok)

    def attend(state, block, back):
        best, mass, acc = state
        kdoc, kpos = docs_of((device - back) * tok)
        kdoc = jnp.where(device - back >= 0, kdoc, -1)
        keys = block[:, 0].reshape(tok, kv_heads, HD)
        values = block[:, 1].reshape(tok, kv_heads, HD)
        scores = (
            jnp.einsum("qgjd,kgd->gjqk", qrows, keys, preferred_element_type=jnp.float32)
            * score_scale
        )
        visible = (qdoc[:, None] == kdoc[None, :]) & (kpos[None, :] <= qpos[:, None])
        scores = jnp.where(visible[None, None], scores, -1e30)
        top = jnp.maximum(best, jnp.max(scores, axis=-1))
        probs = jnp.exp(scores - top[..., None])
        shrink = jnp.exp(best - top)
        mass = mass * shrink + jnp.sum(probs, axis=-1)
        acc = acc * shrink[..., None] + jnp.einsum(
            "gjqk,kgd->gjqd", probs.astype(jnp.bfloat16), values, preferred_element_type=jnp.float32
        )
        return (top, mass, acc)

    state = (
        jnp.full((kv_heads, group, tok), -1e30, jnp.float32),
        jnp.zeros((kv_heads, group, tok), jnp.float32),
        jnp.zeros((kv_heads, group, tok, HD), jnp.float32),
    )
    state = attend(state, kv_local, 0)
    moving = kv_local
    for back in range(1, CYCLE + 1):
        moving = shifted(moving, "ctx", 1)
        state = attend(state, moving, back)
    best, mass, acc = state
    result = acc / mass[..., None]
    return result.transpose(2, 0, 1, 3).reshape(tok, queries.shape[1]).astype(jnp.bfloat16)


def solution(mesh):
    in_specs = (P("ctx", "tp"), P("ctx", "tp"), P(), P("tp"), P(None, None, "tp"), P(None, "tp"))
    out_specs = P("ctx", "tp")
    return jax.shard_map(body, mesh=mesh, in_specs=in_specs, out_specs=out_specs, check_vma=False)
```

profile of v0, /device:TPU:4, one launch (start us, length us, event | category | flops | bytes accessed | tf_op | source)
XLA Modules:
  0.0 223.8 jit_solution(11458401559064904060)
XLA Ops:
  6.5 1.8 fusion.30
  8.3 6.6 %psum.7 = f32[512]{0:T(512)S(1)} all-reduce(f32[512]{0:T(512)S(1)} %fusion.30), channel_id=1, replica_groups=mesh['ctx'=64,'tp'=4] {'tp'}, use_global_device_ids=true, to_apply=%region_4.5 | all-reduce | flops 512 | bytes 4096 | tf_op jit(solution)/shard_map/psum | solution.py:20
  14.9 2.7 %fusion.32 = bf16[512,1280]{1,0:T(8,128)(2,1)} fusion(bf16[512,1280]{1,0:T(8,128)(2,1)} %param.6, f32[1280]{0:T(1024)} %param.9, f32[512]{0:T(512)S(1)} %add_rsqrt_fusion), kind=kLoop, calls=%fused_computation.39 | loop fusion | flops 2621440 | bytes 2628608 | tf_op jit(solution)/shard_map/convert_element_type | solution.py:22
  17.6 0.0 all-gather.2.cloned.1.call-update
  17.7 1.0 reduce-window.9
  18.7 0.1 slice.37
  18.8 5.7 %copy.82 = bf16[640,8,2,256]{3,1,2,0:T(8,128)(2,1)} copy(bf16[640,8,2,256]{3,2,1,0:T(2,128)(2,1)} %bitcast.263) | data formatting | bytes 10485760
  24.5 0.6 copy.35
  25.2 0.1 slice_reduce_fusion
  25.3 0.1 add_bitcast_fusion
  25.4 0.9 convert_reduce_fusion
  26.4 1.4 compare_and_fusion.4
  27.8 49.7 %all-gather.2.cloned.1.call-done = bf16[512,5120]{1,0:T(8,128)(2,1)} async-done(((bf16[512,1280]{1,0:T(8,128)(2,1)}), bf16[512,5120]{1,0:T(8,128)(2,1)}) %all-gather.2.cloned.1.call-update) | async-done | bytes 5242896 | tf_op jit(solution)/shard_map/all_gather | solution.py:25
  77.5 7.0 %fusion.41 = bf16[512,512]{0,1:T(8,128)(2,1)S(1)} fusion(bf16[512,5120]{1,0:T(8,128)(2,1)} %all-gather.2.cloned.1.call-done, bf16[5120,512]{1,0:T(8,128)(2,1)} %bitcast.264, f32[512]{0:T(512)S(1)} %bitcast.279), kind=kOutput, calls=%fused_computation.52 | convolution fusion | flops 2684878848 | bytes 11012096 | tf_op jit(solution)/shard_map/dot_general | solution.py:24
  84.5 3.5 %collective-permute-start = (bf16[512,2,256]{0,2,1:T(8,128)(2,1)S(1)}, bf16[512,2,256]{0,2,1:T(8,128)(2,1)S(1)}, u32[]{:S(2)}, u32[]{:S(2)}) collective-permute-start(bf16[512,2,256]{0,2,1:T(8,128)(2,1)S(1)} %bitcast.271), channel_id=1, source_target_pairs={{0,4},{4,8},{8,12},{12,16},{16,20},{20,24},{24,28},{28,32},{32,36}... | collective-permute-start | bytes 1572872 | tf_op jit(solution)/shard_map/ppermute | solution.py:14
  88.0 0.7 fusion.65
  88.7 1.9 fusion.10
  90.6 16.3 %collective-permute-done = bf16[512,2,256]{0,2,1:T(8,128)(2,1)S(1)} collective-permute-done((bf16[512,2,256]{0,2,1:T(8,128)(2,1)S(1)}, bf16[512,2,256]{0,2,1:T(8,128)(2,1)S(1)}, u32[]{:S(2)}, u32[]{:S(2)}) %collective-permute-start) | collective-permute-done | bytes 524320 | tf_op jit(solution)/shard_map/ppermute | solution.py:14
  106.9 1.9 collective-permute-start.1
  108.8 0.7 fusion.66
  109.6 5.7 %fusion.11 = (f32[2,5,512]{2,1,0:T(8,128)S(1)}, f32[2,512,512,5]{2,1,3,0:T(8,128)}) fusion(pred[512,512]{0,1:T(8,128)(4,1)S(1)} %get-tuple-element.35, bf16[512,2,128,1]{0,2,3,1:T(8,128)(2,1)S(1)} %bitcast.268, bf16[512,2,5,128]{0,3,2,1:T(8,128)(2,1)S(1)} %bitcast.251), kind=kOutput, calls=%fused_computation.21 | convolution fusion | flops 678947840 | bytes 12341248 | tf_op jit(solution)/shard_map/qgjd,kgd->gjqk/dot_general | solution.py:55
  115.3 13.2 %collective-permute-done.1 = bf16[512,2,256]{0,2,1:T(8,128)(2,1)S(1)} collective-permute-done((bf16[512,2,256]{0,2,1:T(8,128)(2,1)S(1)}, bf16[512,2,256]{0,2,1:T(8,128)(2,1)S(1)}, u32[]{:S(2)}, u32[]{:S(2)}) %collective-permute-start.1) | collective-permute-done | bytes 524320 | tf_op jit(solution)/shard_map/ppermute | solution.py:14
  128.5 2.1 collective-permute-start.2
  130.6 0.8 fusion.67
  131.3 5.9 %fusion.12 = (f32[2,5,512]{2,1,0:T(8,128)S(1)}, f32[2,512,512,5]{2,1,3,0:T(8,128)}) fusion(pred[512,512]{0,1:T(8,128)(4,1)S(1)} %get-tuple-element.32, bf16[512,2,128,1]{0,2,3,1:T(8,128)(2,1)S(1)} %bitcast.269, bf16[512,2,5,128]{0,3,2,1:T(8,128)(2,1)S(1)} %bitcast.252), kind=kOutput, calls=%fused_computation.22 | convolution fusion | flops 678947840 | bytes 12341248 | tf_op jit(solution)/shard_map/qgjd,kgd->gjqk/dot_general | solution.py:55
  137.2 12.0 %collective-permute-done.2 = bf16[512,2,256]{0,2,1:T(8,128)(2,1)S(1)} collective-permute-done((bf16[512,2,256]{0,2,1:T(8,128)(2,1)S(1)}, bf16[512,2,256]{0,2,1:T(8,128)(2,1)S(1)}, u32[]{:S(2)}, u32[]{:S(2)}) %collective-permute-start.2) | collective-permute-done | bytes 524320 | tf_op jit(solution)/shard_map/ppermute | solution.py:14
  149.2 1.9 collective-permute-start.3
  151.1 0.7 fusion.68
  151.8 5.9 %fusion.13 = (f32[2,5,512]{2,1,0:T(8,128)S(1)}, f32[2,512,512,5]{2,1,3,0:T(8,128)}) fusion(pred[512,512]{0,1:T(8,128)(4,1)S(1)} %get-tuple-element.33, bf16[512,2,128,1]{0,2,3,1:T(8,128)(2,1)S(1)} %bitcast.270, bf16[512,2,5,128]{0,3,2,1:T(8,128)(2,1)S(1)} %bitcast.253), kind=kOutput, calls=%fused_computation.23 | convolution fusion | flops 678947840 | bytes 12341248 | tf_op jit(solution)/shard_map/qgjd,kgd->gjqk/dot_general | solution.py:55
  157.7 11.3 %collective-permute-done.3 = bf16[512,2,256]{0,2,1:T(8,128)(2,1)S(1)} collective-permute-done((bf16[512,2,256]{0,2,1:T(8,128)(2,1)S(1)}, bf16[512,2,256]{0,2,1:T(8,128)(2,1)S(1)}, u32[]{:S(2)}, u32[]{:S(2)}) %collective-permute-start.3) | collective-permute-done | bytes 524320 | tf_op jit(solution)/shard_map/ppermute | solution.py:14
  169.0 0.7 fusion.64
  169.7 5.7 %fusion.14 = (f32[2,5,512]{2,1,0:T(8,128)S(1)}, f32[2,512,512,5]{2,1,3,0:T(8,128)}) fusion(pred[512,512]{0,1:T(8,128)(4,1)S(1)} %get-tuple-element.34, bf16[512,2,128,1]{0,2,3,1:T(8,128)(2,1)S(1)} %bitcast.266, bf16[512,2,5,128]{0,3,2,1:T(8,128)(2,1)S(1)} %bitcast.254), kind=kOutput, calls=%fused_computation.24 | convolution fusion | flops 678947840 | bytes 12341248 | tf_op jit(solution)/shard_map/qgjd,kgd->gjqk/dot_general | solution.py:55
  175.4 0.6 fusion.62
  176.1 2.2 fusion
  178.3 0.0 slice-start.2
  178.3 5.7 %fusion.23 = f32[2,5,512,128]{2,3,1,0:T(8,128)} fusion(bf16[512,2,128,1]{0,2,3,1:T(8,128)(2,1)} %bitcast.273, f32[2,512,512,5]{2,1,3,0:T(8,128)S(1)} %get-tuple-element.45, f32[2,5,512]{2,1,0:T(8,128)S(1)} %get-tuple-element.30, pred[512,512]{0,1:T(8,128)(4,1)S(1)} %get-tuple-element.31), kind=kOutput, calls=%fused_computation.29 | convolution fusion | flops 681574400 | bytes 13651968 | tf_op jit(solution)/shard_map/gjqk,kgd->gjqd/dot_general | solution.py:64
  184.0 0.0 slice-start.6
  184.0 0.0 slice-start.7
  184.0 3.0 %fusion.2 = f32[2,5,512]{2,1,0:T(8,128)S(1)} fusion(f32[2,512,512,5]{2,1,3,0:T(8,128)S(1)} %bitcast.256, f32[2,5,512]{2,1,0:T(8,128)} %get-tuple-element.17, pred[512,512]{0,1:T(8,128)(4,1)S(1)} %get-tuple-element.35), kind=kLoop, calls=%fused_computation.12 | loop fusion | flops 10480640 | bytes 10788864 | tf_op jit(solution)/shard_map/reduce_sum | solution.py:63
  187.1 0.0 slice-start.8
  187.1 5.0 %fusion.21 = f32[2,5,512,128]{2,3,1,0:T(8,128)} fusion(bf16[512,2,128,1]{0,2,3,1:T(8,128)(2,1)S(1)} %bitcast.275, f32[2,512,512,5]{2,1,3,0:T(8,128)S(1)} %bitcast.256, f32[2,5,512]{2,1,0:T(8,128)} %get-tuple-element.17, pred[512,512]{0,1:T(8,128)(4,1)S(1)} %get-tuple-element.35), kind=kOutput, calls=%fused_computation.28 | convolution fusion | flops 681574400 | bytes 13651968 | tf_op jit(solution)/shard_map/gjqk,kgd->gjqd/dot_general | solution.py:64
  192.1 0.0 slice-done.7
  192.1 0.0 slice-done.8
  192.1 0.0 slice-start.9
  192.1 0.0 slice-start.10
  192.1 3.6 %fusion.4 = f32[2,5,512]{2,1,0:T(8,128)} fusion(f32[2,512,512,5]{2,1,3,0:T(8,128)S(1)} %bitcast.260, f32[2,5,512]{2,1,0:T(8,128)} %get-tuple-element.16, pred[512,512]{0,1:T(8,128)(4,1)S(1)} %get-tuple-element.32), kind=kLoop, calls=%fused_computation.14 | loop fusion | flops 10480640 | bytes 10788864 | tf_op jit(solution)/shard_map/reduce_sum | solution.py:63
  195.8 5.0 %fusion.19 = f32[2,5,512,128]{2,3,1,0:T(8,128)} fusion(bf16[512,2,128,1]{0,2,3,1:T(8,128)(2,1)S(1)} %bitcast.276, f32[2,512,512,5]{2,1,3,0:T(8,128)S(1)} %bitcast.260, f32[2,5,512]{2,1,0:T(8,128)} %get-tuple-element.16, pred[512,512]{0,1:T(8,128)(4,1)S(1)} %get-tuple-element.32), kind=kOutput, calls=%fused_computation.27 | convolution fusion | flops 681574400 | bytes 13651968 | tf_op jit(solution)/shard_map/gjqk,kgd->gjqd/dot_general | solution.py:64
  200.8 0.0 slice-done.9
  200.8 0.0 slice-done.11
  200.8 0.0 slice-start.3
  200.8 0.0 slice-start.4
  200.8 2.2 fusion.6
  203.0 0.0 slice-start.5
  203.0 0.0 copy-start.5
  203.0 0.0 copy-start.1
  203.0 4.0 %fusion.17 = f32[2,5,512,128]{2,3,1,0:T(8,128)} fusion(bf16[512,2,128,1]{0,2,3,1:T(8,128)(2,1)S(1)} %bitcast.277, f32[2,512,512,5]{2,1,3,0:T(8,128)S(1)} %bitcast.262, f32[2,5,512]{2,1,0:T(8,128)S(1)} %get-tuple-element.15, pred[512,512]{0,1:T(8,128)(4,1)S(1)} %get-tuple-element.33), kind=kOutput, calls=%fused_computation.26 | convolution fusion | flops 681574400 | bytes 13651968 | tf_op jit(solution)/shard_map/gjqk,kgd->gjqd/dot_general | solution.py:64
  207.1 0.0 slice-done.3
  207.1 0.0 slice-done.4
  207.1 0.0 slice-done.5
  207.1 2.2 fusion.8
  209.4 0.2 copy-done.8
  209.6 0.8 copy-done.9
  210.4 5.1 %fusion.34 = bf16[512,2,5,128]{0,3,2,1:T(8,128)(2,1)S(1)} fusion(f32[2,5,512,128]{2,3,1,0:T(8,128)} %fusion.17, f32[2,5,512,128]{2,3,1,0:T(8,128)S(1)} %copy-done.9, f32[2,5,512,128]{2,3,1,0:T(8,128)S(1)} %copy-done.8, f32[2,5,512,128]{2,3,1,0:T(8,128)S(1)} %copy-done.7, bf16[512,2,128,1]{0,2,3,1:T(8,128)(2,1)S(1)} %bitcast.274, ...), kind=kOutput, calls=%fused_computation.42 | convolution fusion | flops 688783360 | bytes 22949888 | tf_op jit(solution)/shard_map/gjqk,kgd->gjqd/dot_general | solution.py:64
  215.5 1.4 copy.51
  (41 shorter events, 0.2 us)
Async XLA Ops:
  6.5 18.0 %copy-start.6 = (f32[2,256]{1,0:T(2,128)S(1)}, f32[2,256]{1,0:T(2,128)}, u32[]{:S(2)}) copy-start(f32[2,256]{1,0:T(2,128)} %param.11) | copy-start | bytes 6148
  6.5 18.0 %copy-start = (bf16[512,1280]{1,0:T(8,128)(2,1)S(1)}, bf16[512,1280]{1,0:T(8,128)(2,1)}, u32[]{:S(2)}) copy-start(bf16[512,1280]{1,0:T(8,128)(2,1)} %param.7) | copy-start | bytes 3932164
  6.5 71.0 %all-gather.2.cloned.1.call-start = ((), (), s32[]{:S(2)}) async-start(), calls=%async_computation | async-start | bytes 6553600 | tf_op jit(solution)/shard_map/all_gather | solution.py:25
  84.5 22.4 %collective-permute-start = (bf16[512,2,256]{0,2,1:T(8,128)(2,1)S(1)}, bf16[512,2,256]{0,2,1:T(8,128)(2,1)S(1)}, u32[]{:S(2)}, u32[]{:S(2)}) collective-permute-start(bf16[512,2,256]{0,2,1:T(8,128)(2,1)S(1)} %bitcast.271), channel_id=1, source_target_pairs={{0,4},{4,8},{8,12},{12,16},{16,20},{20,24},{24,28},{28,32},{32,36}... | collective-permute-start | bytes 1572872 | tf_op jit(solution)/shard_map/ppermute | solution.py:14
  106.9 21.5 %collective-permute-start.1 = (bf16[512,2,256]{0,2,1:T(8,128)(2,1)S(1)}, bf16[512,2,256]{0,2,1:T(8,128)(2,1)S(1)}, u32[]{:S(2)}, u32[]{:S(2)}) collective-permute-start(bf16[512,2,256]{0,2,1:T(8,128)(2,1)S(1)} %collective-permute-done), channel_id=1, source_target_pairs={{0,4},{4,8},{8,12},{12,16},{16,20},{20,24},{24,28},{28,32},{32,36}... | collective-permute-start | bytes 1572872 | tf_op jit(solution)/shard_map/ppermute | solution.py:14
  128.5 20.7 %collective-permute-start.2 = (bf16[512,2,256]{0,2,1:T(8,128)(2,1)S(1)}, bf16[512,2,256]{0,2,1:T(8,128)(2,1)S(1)}, u32[]{:S(2)}, u32[]{:S(2)}) collective-permute-start(bf16[512,2,256]{0,2,1:T(8,128)(2,1)S(1)} %collective-permute-done.1), channel_id=1, source_target_pairs={{0,4},{4,8},{8,12},{12,16},{16,20},{20,24},{24,28},{28,32},{32,36}... | collective-permute-start | bytes 1572872 | tf_op jit(solution)/shard_map/ppermute | solution.py:14
  149.2 19.8 %collective-permute-start.3 = (bf16[512,2,256]{0,2,1:T(8,128)(2,1)S(1)}, bf16[512,2,256]{0,2,1:T(8,128)(2,1)S(1)}, u32[]{:S(2)}, u32[]{:S(2)}) collective-permute-start(bf16[512,2,256]{0,2,1:T(8,128)(2,1)S(1)} %collective-permute-done.2), channel_id=1, source_target_pairs={{0,4},{4,8},{8,12},{12,16},{16,20},{20,24},{24,28},{28,32},{32,36}... | collective-permute-start | bytes 1572872 | tf_op jit(solution)/shard_map/ppermute | solution.py:14
  176.1 7.9 %slice-start = ((s8[10485760]{0:T(1024)(128)(4,1)}), s8[4194304]{0:T(1024)(128)(4,1)S(1)}, s32[]{:S(2)}) async-start(s8[10485760]{0:T(1024)(128)(4,1)} %bitcast.255), calls=%async_computation.1 | async-start | bytes 8388608
  176.1 7.9 %slice-start.1 = ((s8[10485760]{0:T(1024)(128)(4,1)}), s8[4194304]{0:T(1024)(128)(4,1)S(1)}, s32[]{:S(2)}) async-start(s8[10485760]{0:T(1024)(128)(4,1)} %bitcast.255), calls=%async_computation.2 | async-start | bytes 8388608
  178.3 5.7 %slice-start.2 = ((s8[10485760]{0:T(1024)(128)(4,1)}), s8[2097152]{0:T(1024)(128)(4,1)S(1)}, s32[]{:S(2)}) async-start(s8[10485760]{0:T(1024)(128)(4,1)} %bitcast.255), calls=%async_computation.3 | async-start | bytes 4194304
  183.9 3.1 %copy-start.2 = (bf16[512,1,256]{0,2,1:T(8,128)(2,1)S(1)}, bf16[512,1,256]{0,2,1:T(8,128)(2,1)}, u32[]{:S(2)}) copy-start(bf16[512,1,256]{0,2,1:T(8,128)(2,1)} %get-tuple-element.22) | copy-start | bytes 786436
  184.0 8.1 %slice-start.6 = ((s8[10485760]{0:T(1024)(128)(4,1)}), s8[4194304]{0:T(1024)(128)(4,1)S(1)}, s32[]{:S(2)}) async-start(s8[10485760]{0:T(1024)(128)(4,1)} %bitcast.259), calls=%async_computation.7 | async-start | bytes 8388608
  184.0 8.1 %slice-start.7 = ((s8[10485760]{0:T(1024)(128)(4,1)}), s8[4194304]{0:T(1024)(128)(4,1)S(1)}, s32[]{:S(2)}) async-start(s8[10485760]{0:T(1024)(128)(4,1)} %bitcast.259), calls=%async_computation.8 | async-start | bytes 8388608
  187.1 5.0 %slice-start.8 = ((s8[10485760]{0:T(1024)(128)(4,1)}), s8[2097152]{0:T(1024)(128)(4,1)S(1)}, s32[]{:S(2)}) async-start(s8[10485760]{0:T(1024)(128)(4,1)} %bitcast.259), calls=%async_computation.9 | async-start | bytes 4194304
  192.1 3.7 %copy-start.3 = (bf16[512,1,256]{0,2,1:T(8,128)(2,1)S(1)}, bf16[512,1,256]{0,2,1:T(8,128)(2,1)}, u32[]{:S(2)}) copy-start(bf16[512,1,256]{0,2,1:T(8,128)(2,1)} %get-tuple-element.24) | copy-start | bytes 786436
  192.1 8.7 %slice-start.9 = ((s8[10485760]{0:T(1024)(128)(4,1)}), s8[4194304]{0:T(1024)(128)(4,1)S(1)}, s32[]{:S(2)}) async-start(s8[10485760]{0:T(1024)(128)(4,1)} %bitcast.261), calls=%async_computation.10 | async-start | bytes 8388608
  192.1 8.7 %slice-start.10 = ((s8[10485760]{0:T(1024)(128)(4,1)}), s8[4194304]{0:T(1024)(128)(4,1)S(1)}, s32[]{:S(2)}) async-start(s8[10485760]{0:T(1024)(128)(4,1)} %bitcast.261), calls=%async_computation.11 | async-start | bytes 8388608
  195.8 5.0 %slice-start.11 = ((s8[10485760]{0:T(1024)(128)(4,1)}), s8[2097152]{0:T(1024)(128)(4,1)S(1)}, s32[]{:S(2)}) async-start(s8[10485760]{0:T(1024)(128)(4,1)} %bitcast.261), calls=%async_computation.12 | async-start | bytes 4194304
  195.8 7.2 %copy-start.4 = (bf16[512,1,256]{0,2,1:T(8,128)(2,1)S(1)}, bf16[512,1,256]{0,2,1:T(8,128)(2,1)}, u32[]{:S(2)}) copy-start(bf16[512,1,256]{0,2,1:T(8,128)(2,1)} %get-tuple-element.27) | copy-start | bytes 786436
  200.8 6.3 %slice-start.3 = ((s8[10485760]{0:T(1024)(128)(4,1)}), s8[4194304]{0:T(1024)(128)(4,1)S(1)}, s32[]{:S(2)}) async-start(s8[10485760]{0:T(1024)(128)(4,1)} %bitcast.257), calls=%async_computation.4 | async-start | bytes 8388608
  200.8 6.3 %slice-start.4 = ((s8[10485760]{0:T(1024)(128)(4,1)}), s8[4194304]{0:T(1024)(128)(4,1)S(1)}, s32[]{:S(2)}) async-start(s8[10485760]{0:T(1024)(128)(4,1)} %bitcast.257), calls=%async_computation.5 | async-start | bytes 8388608
  203.0 4.1 %slice-start.5 = ((s8[10485760]{0:T(1024)(128)(4,1)}), s8[2097152]{0:T(1024)(128)(4,1)S(1)}, s32[]{:S(2)}) async-start(s8[10485760]{0:T(1024)(128)(4,1)} %bitcast.257), calls=%async_computation.6 | async-start | bytes 4194304
  203.0 6.3 %copy-start.5 = (f32[2,5,512]{2,1,0:T(8,128)S(1)}, f32[2,5,512]{2,1,0:T(8,128)}, u32[]{:S(2)}) copy-start(f32[2,5,512]{2,1,0:T(8,128)} %fusion.4) | copy-start | bytes 61444
  203.0 6.4 %copy-start.1 = (bf16[512,1,256]{0,2,1:T(8,128)(2,1)S(1)}, bf16[512,1,256]{0,2,1:T(8,128)(2,1)}, u32[]{:S(2)}) copy-start(bf16[512,1,256]{0,2,1:T(8,128)(2,1)} %get-tuple-element.18) | copy-start | bytes 786436
  207.1 2.3 %copy-start.7 = (f32[2,5,512,128]{2,3,1,0:T(8,128)S(1)}, f32[2,5,512,128]{2,3,1,0:T(8,128)}, u32[]{:S(2)}) copy-start(f32[2,5,512,128]{2,3,1,0:T(8,128)} %fusion.23) | copy-start | bytes 7864324
  207.1 2.5 %copy-start.8 = (f32[2,5,512,128]{2,3,1,0:T(8,128)S(1)}, f32[2,5,512,128]{2,3,1,0:T(8,128)}, u32[]{:S(2)}) copy-start(f32[2,5,512,128]{2,3,1,0:T(8,128)} %fusion.21) | copy-start | bytes 7864324
  207.1 3.3 %copy-start.9 = (f32[2,5,512,128]{2,3,1,0:T(8,128)S(1)}, f32[2,5,512,128]{2,3,1,0:T(8,128)}, u32[]{:S(2)}) copy-start(f32[2,5,512,128]{2,3,1,0:T(8,128)} %fusion.19) | copy-start | bytes 7864324
Sparse Core Ops, SparseCore 0:
  17.8 59.6 all-gather.1
where the time goes:
time: 224 us
  waiting for transfers between devices  102 us (46%)
  matrix products  56.9 us (25%)
  other arithmetic  21.9 us (10%)
  between operations  13.8 us (6%)
  local copies, waits for them, and re-layouts  12.8 us (6%)
  starting transfers between devices  9.37 us (4%)
  blocking collectives  6.6 us (3%)
    ppermute x4, waiting for transfers between devices, shifted(): lax.ppermute(value, axis, [(source, source + steps) for source in range(l...  52.7 us
    all_gather x1, waiting for transfers between devices, body(): lax.all_gather(normed, 'tp', axis=1, tiled=True)  49.7 us
    dot_general x5, matrix products, attend(): jnp.einsum('qgjd,kgd->gjqk', qrows, keys, preferred_element_type=jnp.floa...  25.1 us
    dot_general x5, matrix products, attend(): jnp.einsum('gjqk,kgd->gjqd', probs.astype(jnp.bfloat16), values, preferre...  24.8 us
    reduce_sum x5, other arithmetic, attend(): mass = mass * shrink + jnp.sum(probs, axis=-1)  13.2 us
    ppermute x4, starting transfers between devices, shifted(): lax.ppermute(value, axis, [(source, source + steps) for source in range(l...  9.37 us
    unnamed x47, local copies, waits for them, and re-layouts  7.45 us
    dot_general x1, matrix products, body(): jnp.dot(lax.all_gather(normed, 'tp', axis=1, tiled=True), flat_weight, pr...  6.97 us
  transfers between devices with their start and end apart: 5, of which 5 were waited for; matrix products, arithmetic and copies ran while one was open for 14% of the time, Pallas kernels for 0%

commit v1 on v0

--- a/solution.py
+++ b/solution.py
@@ -6,6 +6,13 @@
 D = 5120
 HD = 128
 CYCLE = 4
+
+
+def close_lots_all(arr_in, dim_no):
+    return jnp.concatenate(
+        lax.all_to_all(jnp.stack([arr_in for _ in range(lax.axis_size("tp"))]), "tp", 0, 0),
+        axis=dim_no,
+    )
 
 
 def shifted(value, axis, steps):
@@ -21,11 +28,7 @@
     scale_rows = lax.rsqrt(squares / D + 1e-06)
     normed = (xfull * scale_rows[:, None] * norm_gain[None, :]).astype(jnp.bfloat16)
     flat_weight = kv_weight.reshape(kv_weight.shape[0], -1)
-    summed = jnp.dot(
-        lax.all_gather(normed, "tp", axis=1, tiled=True),
-        flat_weight,
-        preferred_element_type=jnp.float32,
-    )
+    summed = jnp.dot(close_lots_all(normed, 1), flat_weight, preferred_element_type=jnp.float32)
     kv_local = (
         (summed + kv_bias.reshape(-1)[None, :])
         .astype(jnp.bfloat16)

time: 224 us -> 215 us (0.960)
  between operations: 13.8 us -> 0.45 us
  starting transfers between devices: 9.37 us -> 14.9 us
  local copies, waits for them, and re-layouts: 12.8 us -> 16.2 us
  waiting for transfers between devices: 102 us -> 98.8 us
    all_to_all x0 -> x1, waiting for transfers between devices: none -> 50 us  [close_lots_all(): lax.all_to_all(jnp.stack([arr_in for _ in range(lax.axis_size('tp'))]), '...]
    all_gather x1 -> x0, waiting for transfers between devices: 49.7 us -> none  [body(): lax.all_gather(normed, 'tp', axis=1, tiled=True)]
    all_to_all x0 -> x1, starting transfers between devices: none -> 5.17 us  [close_lots_all(): lax.all_to_all(jnp.stack([arr_in for _ in range(lax.axis_size('tp'))]), '...]
    ppermute x4, waiting for transfers between devices: 52.7 us -> 48.8 us  [shifted(): lax.ppermute(value, axis, [(source, source + steps) for source in range(l...]
    another operation x1 -> x2, local copies, waits for them, and re-layouts: 0.11 us -> 2.88 us  [the longest x1 2.77 us: close_lots_all(): jnp.stack([arr_in for _ in range(lax.axis_size('tp'))])]
    unnamed x47 -> x49, local copies, waits for them, and re-layouts: 7.45 us -> 7.48 us
  transfers between devices with their start and end apart: 5 -> 5, of which waited for: 5 -> 5; matrix products, arithmetic and copies ran while one was open for 14% -> 15% of each run, Pallas kernels for 0% -> 0%
where the time goes in v1:
time: 215 us; the launch traced here: 214 us
  waiting for transfers between devices  98.8 us (46%)
  matrix products  56.9 us (26%)
  other arithmetic  20.1 us (9%)
  local copies, waits for them, and re-layouts  16.2 us (8%)
  starting transfers between devices  14.9 us (7%)
  blocking collectives  6.6 us (3%)
    all_to_all x1, waiting for transfers between devices, close_lots_all(): lax.all_to_all(jnp.stack([arr_in for _ in range(lax.axis_size('tp'))]), '...  50 us
    ppermute x4, waiting for transfers between devices, shifted(): lax.ppermute(value, axis, [(source, source + steps) for source in range(l...  48.8 us
    dot_general x5, matrix products, attend(): jnp.einsum('qgjd,kgd->gjqk', qrows, keys, preferred_element_type=jnp.floa...  25.1 us
    dot_general x5, matrix products, attend(): jnp.einsum('gjqk,kgd->gjqd', probs.astype(jnp.bfloat16), values, preferre...  24.8 us
    reduce_sum x5, other arithmetic, attend(): mass = mass * shrink + jnp.sum(probs, axis=-1)  13.2 us
    ppermute x4, starting transfers between devices, shifted(): lax.ppermute(value, axis, [(source, source + steps) for source in range(l...  9.73 us
    unnamed x49, local copies, waits for them, and re-layouts  7.48 us
    dot_general x1, matrix products, body(): jnp.dot(close_lots_all(normed, 1), flat_weight, preferred_element_type=jn...  6.97 us
  transfers between devices with their start and end apart: 5, of which 5 were waited for; matrix products, arithmetic and copies ran while one was open for 15% of the time, Pallas kernels for 0%

profile of v1, /device:TPU:4, one launch (start us, length us, event | category | flops | bytes accessed | tf_op | source)
XLA Modules:
  0.0 213.9 jit_solution(11692860898690413542)
XLA Ops:
  0.0 1.6 fusion.30
  1.6 6.6 %psum.7 = f32[512]{0:T(512)S(1)} all-reduce(f32[512]{0:T(512)S(1)} %fusion.30), channel_id=1, replica_groups=mesh['ctx'=64,'tp'=4] {'tp'}, use_global_device_ids=true, to_apply=%region_4.5 | all-reduce | flops 512 | bytes 4096 | tf_op jit(solution)/shard_map/psum | solution.py:27
  8.3 1.7 fusion.32
  9.9 0.0 copy-start.7
  10.0 0.7 copy.36
  10.6 2.8 %stack.2 = bf16[4,512,1280]{1,2,0:T(8,128)(2,1)} broadcast(bf16[512,1280]{0,1:T(8,128)(2,1)S(1)} %copy.36), dimensions={1,2} | broadcast | bytes 6553600 | tf_op jit(solution)/shard_map/stack | solution.py:13
  13.4 5.2 %all-to-all-start = ((bf16[4,512,1280]{1,2,0:T(8,128)(2,1)}), bf16[4,512,1280]{1,2,0:T(8,128)(2,1)}, u32[]{:S(2)}, u32[]{:S(2)}) async-start(bf16[4,512,1280]{1,2,0:T(8,128)(2,1)} %stack.2), calls=%async_computation | async-start | bytes 10485760 | tf_op jit(solution)/shard_map/all_to_all | solution.py:13
  18.6 0.0 copy-done.7
  18.6 0.3 reduce-window.9
  18.9 0.1 slice.37
  19.0 5.7 %copy.84 = bf16[640,8,2,256]{3,1,2,0:T(8,128)(2,1)} copy(bf16[640,8,2,256]{3,2,1,0:T(2,128)(2,1)} %bitcast.266) | data formatting | bytes 10485760
  24.8 0.6 copy.37
  25.5 0.1 slice_reduce_fusion
  25.6 0.1 add_bitcast_fusion
  25.7 0.9 convert_reduce_fusion
  26.6 1.4 compare_and_fusion.4
  28.1 50.0 %all-to-all-done = bf16[4,512,1280]{1,2,0:T(8,128)(2,1)} async-done(((bf16[4,512,1280]{1,2,0:T(8,128)(2,1)}), bf16[4,512,1280]{1,2,0:T(8,128)(2,1)}, u32[]{:S(2)}, u32[]{:S(2)}) %all-to-all-start) | async-done | bytes 5242912 | tf_op jit(solution)/shard_map/all_to_all | solution.py:13
  78.0 7.0 %fusion.41 = bf16[512,512]{0,1:T(8,128)(2,1)S(1)} fusion(bf16[512,5120]{0,1:T(8,128)(2,1)} %bitcast.3, bf16[5120,512]{1,0:T(8,128)(2,1)} %bitcast.267, f32[512]{0:T(512)S(1)} %bitcast.282), kind=kOutput, calls=%fused_computation.52 | convolution fusion | flops 2684878848 | bytes 11012096 | tf_op jit(solution)/shard_map/dot_general | solution.py:31
  85.0 3.8 %collective-permute-start = (bf16[512,2,256]{0,2,1:T(8,128)(2,1)S(1)}, bf16[512,2,256]{0,2,1:T(8,128)(2,1)S(1)}, u32[]{:S(2)}, u32[]{:S(2)}) collective-permute-start(bf16[512,2,256]{0,2,1:T(8,128)(2,1)S(1)} %bitcast.274), channel_id=1, source_target_pairs={{0,4},{4,8},{8,12},{12,16},{16,20},{20,24},{24,28},{28,32},{32,36}... | collective-permute-start | bytes 1572872 | tf_op jit(solution)/shard_map/ppermute | solution.py:21
  88.8 0.7 fusion.65
  89.6 1.9 fusion.10
  91.5 15.7 %collective-permute-done = bf16[512,2,256]{0,2,1:T(8,128)(2,1)S(1)} collective-permute-done((bf16[512,2,256]{0,2,1:T(8,128)(2,1)S(1)}, bf16[512,2,256]{0,2,1:T(8,128)(2,1)S(1)}, u32[]{:S(2)}, u32[]{:S(2)}) %collective-permute-start) | collective-permute-done | bytes 524320 | tf_op jit(solution)/shard_map/ppermute | solution.py:21
  107.2 1.9 collective-permute-start.1
  109.1 0.7 fusion.66
  109.8 5.7 %fusion.11 = (f32[2,5,512]{2,1,0:T(8,128)S(1)}, f32[2,512,512,5]{2,1,3,0:T(8,128)}) fusion(pred[512,512]{0,1:T(8,128)(4,1)S(1)} %get-tuple-element.35, bf16[512,2,128,1]{0,2,3,1:T(8,128)(2,1)S(1)} %bitcast.271, bf16[512,2,5,128]{0,3,2,1:T(8,128)(2,1)S(1)} %bitcast.254), kind=kOutput, calls=%fused_computation.21 | convolution fusion | flops 678947840 | bytes 12341248 | tf_op jit(solution)/shard_map/qgjd,kgd->gjqk/dot_general | solution.py:58
  115.5 12.1 %collective-permute-done.1 = bf16[512,2,256]{0,2,1:T(8,128)(2,1)S(1)} collective-permute-done((bf16[512,2,256]{0,2,1:T(8,128)(2,1)S(1)}, bf16[512,2,256]{0,2,1:T(8,128)(2,1)S(1)}, u32[]{:S(2)}, u32[]{:S(2)}) %collective-permute-start.1) | collective-permute-done | bytes 524320 | tf_op jit(solution)/shard_map/ppermute | solution.py:21
  127.7 2.1 collective-permute-start.2
  129.8 0.8 fusion.67
  130.5 5.9 %fusion.12 = (f32[2,5,512]{2,1,0:T(8,128)S(1)}, f32[2,512,512,5]{2,1,3,0:T(8,128)}) fusion(pred[512,512]{0,1:T(8,128)(4,1)S(1)} %get-tuple-element.32, bf16[512,2,128,1]{0,2,3,1:T(8,128)(2,1)S(1)} %bitcast.272, bf16[512,2,5,128]{0,3,2,1:T(8,128)(2,1)S(1)} %bitcast.255), kind=kOutput, calls=%fused_computation.22 | convolution fusion | flops 678947840 | bytes 12341248 | tf_op jit(solution)/shard_map/qgjd,kgd->gjqk/dot_general | solution.py:58
  136.4 10.9 %collective-permute-done.2 = bf16[512,2,256]{0,2,1:T(8,128)(2,1)S(1)} collective-permute-done((bf16[512,2,256]{0,2,1:T(8,128)(2,1)S(1)}, bf16[512,2,256]{0,2,1:T(8,128)(2,1)S(1)}, u32[]{:S(2)}, u32[]{:S(2)}) %collective-permute-start.2) | collective-permute-done | bytes 524320 | tf_op jit(solution)/shard_map/ppermute | solution.py:21
  147.2 1.9 collective-permute-start.3
  149.2 0.7 fusion.68
  149.9 5.9 %fusion.13 = (f32[2,5,512]{2,1,0:T(8,128)S(1)}, f32[2,512,512,5]{2,1,3,0:T(8,128)}) fusion(pred[512,512]{0,1:T(8,128)(4,1)S(1)} %get-tuple-element.33, bf16[512,2,128,1]{0,2,3,1:T(8,128)(2,1)S(1)} %bitcast.273, bf16[512,2,5,128]{0,3,2,1:T(8,128)(2,1)S(1)} %bitcast.256), kind=kOutput, calls=%fused_computation.23 | convolution fusion | flops 678947840 | bytes 12341248 | tf_op jit(solution)/shard_map/qgjd,kgd->gjqk/dot_general | solution.py:58
  155.8 10.1 %collective-permute-done.3 = bf16[512,2,256]{0,2,1:T(8,128)(2,1)S(1)} collective-permute-done((bf16[512,2,256]{0,2,1:T(8,128)(2,1)S(1)}, bf16[512,2,256]{0,2,1:T(8,128)(2,1)S(1)}, u32[]{:S(2)}, u32[]{:S(2)}) %collective-permute-start.3) | collective-permute-done | bytes 524320 | tf_op jit(solution)/shard_map/ppermute | solution.py:21
  165.9 0.7 fusion.64
  166.6 5.7 %fusion.14 = (f32[2,5,512]{2,1,0:T(8,128)S(1)}, f32[2,512,512,5]{2,1,3,0:T(8,128)}) fusion(pred[512,512]{0,1:T(8,128)(4,1)S(1)} %get-tuple-element.34, bf16[512,2,128,1]{0,2,3,1:T(8,128)(2,1)S(1)} %bitcast.269, bf16[512,2,5,128]{0,3,2,1:T(8,128)(2,1)S(1)} %bitcast.257), kind=kOutput, calls=%fused_computation.24 | convolution fusion | flops 678947840 | bytes 12341248 | tf_op jit(solution)/shard_map/qgjd,kgd->gjqk/dot_general | solution.py:58
  172.4 0.6 fusion.62
  173.0 2.2 %fusion = f32[2,5,512]{2,1,0:T(8,128)S(1)} fusion(f32[2,512,512,5]{2,1,3,0:T(8,128)S(1)} %get-tuple-element.45, f32[2,5,512]{2,1,0:T(8,128)S(1)} %get-tuple-element.30, pred[512,512]{0,1:T(8,128)(4,1)S(1)} %get-tuple-element.31), kind=kLoop, calls=%fused_computation.10 | loop fusion | flops 10480640 | bytes 10788864 | tf_op jit(solution)/shard_map/reduce_sum | solution.py:66
  175.2 0.0 slice-start.2
  175.2 5.7 %fusion.23 = f32[2,5,512,128]{2,3,1,0:T(8,128)} fusion(bf16[512,2,128,1]{0,2,3,1:T(8,128)(2,1)} %bitcast.276, f32[2,512,512,5]{2,1,3,0:T(8,128)S(1)} %get-tuple-element.45, f32[2,5,512]{2,1,0:T(8,128)S(1)} %get-tuple-element.30, pred[512,512]{0,1:T(8,128)(4,1)S(1)} %get-tuple-element.31), kind=kOutput, calls=%fused_computation.29 | convolution fusion | flops 681574400 | bytes 13651968 | tf_op jit(solution)/shard_map/gjqk,kgd->gjqd/dot_general | solution.py:67
  180.9 0.0 slice-done.1
  180.9 0.0 slice-start.6
  180.9 0.0 slice-start.7
  180.9 3.0 %fusion.2 = f32[2,5,512]{2,1,0:T(8,128)S(1)} fusion(f32[2,512,512,5]{2,1,3,0:T(8,128)S(1)} %bitcast.259, f32[2,5,512]{2,1,0:T(8,128)} %get-tuple-element.17, pred[512,512]{0,1:T(8,128)(4,1)S(1)} %get-tuple-element.35), kind=kLoop, calls=%fused_computation.12 | loop fusion | flops 10480640 | bytes 10788864 | tf_op jit(solution)/shard_map/reduce_sum | solution.py:66
  184.0 0.0 slice-start.8
  184.0 5.0 %fusion.21 = f32[2,5,512,128]{2,3,1,0:T(8,128)} fusion(bf16[512,2,128,1]{0,2,3,1:T(8,128)(2,1)S(1)} %bitcast.278, f32[2,512,512,5]{2,1,3,0:T(8,128)S(1)} %bitcast.259, f32[2,5,512]{2,1,0:T(8,128)} %get-tuple-element.17, pred[512,512]{0,1:T(8,128)(4,1)S(1)} %get-tuple-element.35), kind=kOutput, calls=%fused_computation.28 | convolution fusion | flops 681574400 | bytes 13651968 | tf_op jit(solution)/shard_map/gjqk,kgd->gjqd/dot_general | solution.py:67
  189.0 0.0 slice-done.8
  189.0 0.0 slice-start.9
  189.0 0.0 slice-start.10
  189.0 3.6 %fusion.4 = f32[2,5,512]{2,1,0:T(8,128)} fusion(f32[2,512,512,5]{2,1,3,0:T(8,128)S(1)} %bitcast.263, f32[2,5,512]{2,1,0:T(8,128)} %get-tuple-element.16, pred[512,512]{0,1:T(8,128)(4,1)S(1)} %get-tuple-element.32), kind=kLoop, calls=%fused_computation.14 | loop fusion | flops 10480640 | bytes 10788864 | tf_op jit(solution)/shard_map/reduce_sum | solution.py:66
  192.7 5.0 %fusion.19 = f32[2,5,512,128]{2,3,1,0:T(8,128)} fusion(bf16[512,2,128,1]{0,2,3,1:T(8,128)(2,1)S(1)} %bitcast.279, f32[2,512,512,5]{2,1,3,0:T(8,128)S(1)} %bitcast.263, f32[2,5,512]{2,1,0:T(8,128)} %get-tuple-element.16, pred[512,512]{0,1:T(8,128)(4,1)S(1)} %get-tuple-element.32), kind=kOutput, calls=%fused_computation.27 | convolution fusion | flops 681574400 | bytes 13651968 | tf_op jit(solution)/shard_map/gjqk,kgd->gjqd/dot_general | solution.py:67
  197.7 0.0 slice-done.11
  197.7 0.0 slice-start.3
  197.7 0.0 slice-start.4
  197.7 2.2 %fusion.6 = f32[2,5,512]{2,1,0:T(8,128)S(1)} fusion(f32[2,512,512,5]{2,1,3,0:T(8,128)S(1)} %bitcast.265, f32[2,5,512]{2,1,0:T(8,128)S(1)} %get-tuple-element.15, pred[512,512]{0,1:T(8,128)(4,1)S(1)} %get-tuple-element.33), kind=kLoop, calls=%fused_computation.16 | loop fusion | flops 10480640 | bytes 10788864 | tf_op jit(solution)/shard_map/reduce_sum | solution.py:66
  199.9 0.0 slice-start.5
  199.9 4.0 %fusion.17 = f32[2,5,512,128]{2,3,1,0:T(8,128)} fusion(bf16[512,2,128,1]{0,2,3,1:T(8,128)(2,1)S(1)} %bitcast.280, f32[2,512,512,5]{2,1,3,0:T(8,128)S(1)} %bitcast.265, f32[2,5,512]{2,1,0:T(8,128)S(1)} %get-tuple-element.15, pred[512,512]{0,1:T(8,128)(4,1)S(1)} %get-tuple-element.33), kind=kOutput, calls=%fused_computation.26 | convolution fusion | flops 681574400 | bytes 13651968 | tf_op jit(solution)/shard_map/gjqk,kgd->gjqd/dot_general | solution.py:67
  204.0 0.0 slice-done.4
  204.0 0.0 slice-done.5
  204.0 2.2 %fusion.8 = f32[2,5,512]{2,1,0:T(8,128)S(1)} fusion(f32[2,512,512,5]{2,1,3,0:T(8,128)S(1)} %bitcast.261, f32[2,5,512]{2,1,0:T(8,128)S(1)} %get-tuple-element.14, pred[512,512]{0,1:T(8,128)(4,1)S(1)} %get-tuple-element.34), kind=kLoop, calls=%fused_computation.18 | loop fusion | flops 10480640 | bytes 10788864 | tf_op jit(solution)/shard_map/reduce_sum | solution.py:66
  206.3 0.2 copy-done.9
  206.5 0.8 copy-done.10
  207.3 5.1 %fusion.34 = bf16[512,2,5,128]{0,3,2,1:T(8,128)(2,1)S(1)} fusion(f32[2,5,512,128]{2,3,1,0:T(8,128)} %fusion.17, f32[2,5,512,128]{2,3,1,0:T(8,128)S(1)} %copy-done.10, f32[2,5,512,128]{2,3,1,0:T(8,128)S(1)} %copy-done.9, f32[2,5,512,128]{2,3,1,0:T(8,128)S(1)} %copy-done.8, bf16[512,2,128,1]{0,2,3,1:T(8,128)(2,1)S(1)} %bitcast.277, ...), kind=kOutput, calls=%fused_computation.42 | convolution fusion | flops 688783360 | bytes 22949888 | tf_op jit(solution)/shard_map/gjqk,kgd->gjqd/dot_general | solution.py:67
  212.4 1.4 copy.53
  (44 shorter events, 0.2 us)
Async XLA Ops:
  9.9 8.7 %copy-start.7 = (s32[256]{0:T(256)S(1)}, s32[256]{0:T(256)}, u32[]{:S(2)}) copy-start(s32[256]{0:T(256)} %param.8) | copy-start | bytes 3076
  13.4 11.4 %copy-start.6 = (f32[2,256]{1,0:T(2,128)S(1)}, f32[2,256]{1,0:T(2,128)}, u32[]{:S(2)}) copy-start(f32[2,256]{1,0:T(2,128)} %param.11) | copy-start | bytes 6148
  13.4 11.4 %copy-start = (bf16[512,1280]{1,0:T(8,128)(2,1)S(1)}, bf16[512,1280]{1,0:T(8,128)(2,1)}, u32[]{:S(2)}) copy-start(bf16[512,1280]{1,0:T(8,128)(2,1)} %param.7) | copy-start | bytes 3932164
  13.4 64.6 %all-to-all-start = ((bf16[4,512,1280]{1,2,0:T(8,128)(2,1)}), bf16[4,512,1280]{1,2,0:T(8,128)(2,1)}, u32[]{:S(2)}, u32[]{:S(2)}) async-start(bf16[4,512,1280]{1,2,0:T(8,128)(2,1)} %stack.2), calls=%async_computation | async-start | bytes 10485760 | tf_op jit(solution)/shard_map/all_to_all | solution.py:13
  85.0 22.2 %collective-permute-start = (bf16[512,2,256]{0,2,1:T(8,128)(2,1)S(1)}, bf16[512,2,256]{0,2,1:T(8,128)(2,1)S(1)}, u32[]{:S(2)}, u32[]{:S(2)}) collective-permute-start(bf16[512,2,256]{0,2,1:T(8,128)(2,1)S(1)} %bitcast.274), channel_id=1, source_target_pairs={{0,4},{4,8},{8,12},{12,16},{16,20},{20,24},{24,28},{28,32},{32,36}... | collective-permute-start | bytes 1572872 | tf_op jit(solution)/shard_map/ppermute | solution.py:21
  107.2 20.5 %collective-permute-start.1 = (bf16[512,2,256]{0,2,1:T(8,128)(2,1)S(1)}, bf16[512,2,256]{0,2,1:T(8,128)(2,1)S(1)}, u32[]{:S(2)}, u32[]{:S(2)}) collective-permute-start(bf16[512,2,256]{0,2,1:T(8,128)(2,1)S(1)} %collective-permute-done), channel_id=1, source_target_pairs={{0,4},{4,8},{8,12},{12,16},{16,20},{20,24},{24,28},{28,32},{32,36}... | collective-permute-start | bytes 1572872 | tf_op jit(solution)/shard_map/ppermute | solution.py:21
  127.7 19.6 %collective-permute-start.2 = (bf16[512,2,256]{0,2,1:T(8,128)(2,1)S(1)}, bf16[512,2,256]{0,2,1:T(8,128)(2,1)S(1)}, u32[]{:S(2)}, u32[]{:S(2)}) collective-permute-start(bf16[512,2,256]{0,2,1:T(8,128)(2,1)S(1)} %collective-permute-done.1), channel_id=1, source_target_pairs={{0,4},{4,8},{8,12},{12,16},{16,20},{20,24},{24,28},{28,32},{32,36}... | collective-permute-start | bytes 1572872 | tf_op jit(solution)/shard_map/ppermute | solution.py:21
  147.2 18.6 %collective-permute-start.3 = (bf16[512,2,256]{0,2,1:T(8,128)(2,1)S(1)}, bf16[512,2,256]{0,2,1:T(8,128)(2,1)S(1)}, u32[]{:S(2)}, u32[]{:S(2)}) collective-permute-start(bf16[512,2,256]{0,2,1:T(8,128)(2,1)S(1)} %collective-permute-done.2), channel_id=1, source_target_pairs={{0,4},{4,8},{8,12},{12,16},{16,20},{20,24},{24,28},{28,32},{32,36}... | collective-permute-start | bytes 1572872 | tf_op jit(solution)/shard_map/ppermute | solution.py:21
  173.0 7.9 %slice-start = ((s8[10485760]{0:T(1024)(128)(4,1)}), s8[4194304]{0:T(1024)(128)(4,1)S(1)}, s32[]{:S(2)}) async-start(s8[10485760]{0:T(1024)(128)(4,1)} %bitcast.258), calls=%async_computation.1 | async-start | bytes 8388608
  173.0 7.9 %slice-start.1 = ((s8[10485760]{0:T(1024)(128)(4,1)}), s8[4194304]{0:T(1024)(128)(4,1)S(1)}, s32[]{:S(2)}) async-start(s8[10485760]{0:T(1024)(128)(4,1)} %bitcast.258), calls=%async_computation.2 | async-start | bytes 8388608
  175.2 5.7 %slice-start.2 = ((s8[10485760]{0:T(1024)(128)(4,1)}), s8[2097152]{0:T(1024)(128)(4,1)S(1)}, s32[]{:S(2)}) async-start(s8[10485760]{0:T(1024)(128)(4,1)} %bitcast.258), calls=%async_computation.3 | async-start | bytes 4194304
  180.9 3.1 %copy-start.2 = (bf16[512,1,256]{0,2,1:T(8,128)(2,1)S(1)}, bf16[512,1,256]{0,2,1:T(8,128)(2,1)}, u32[]{:S(2)}) copy-start(bf16[512,1,256]{0,2,1:T(8,128)(2,1)} %get-tuple-element.22) | copy-start | bytes 786436
  180.9 8.1 %slice-start.6 = ((s8[10485760]{0:T(1024)(128)(4,1)}), s8[4194304]{0:T(1024)(128)(4,1)S(1)}, s32[]{:S(2)}) async-start(s8[10485760]{0:T(1024)(128)(4,1)} %bitcast.262), calls=%async_computation.7 | async-start | bytes 8388608
  180.9 8.1 %slice-start.7 = ((s8[10485760]{0:T(1024)(128)(4,1)}), s8[4194304]{0:T(1024)(128)(4,1)S(1)}, s32[]{:S(2)}) async-start(s8[10485760]{0:T(1024)(128)(4,1)} %bitcast.262), calls=%async_computation.8 | async-start | bytes 8388608
  184.0 5.0 %slice-start.8 = ((s8[10485760]{0:T(1024)(128)(4,1)}), s8[2097152]{0:T(1024)(128)(4,1)S(1)}, s32[]{:S(2)}) async-start(s8[10485760]{0:T(1024)(128)(4,1)} %bitcast.262), calls=%async_computation.9 | async-start | bytes 4194304
  189.0 3.7 %copy-start.3 = (bf16[512,1,256]{0,2,1:T(8,128)(2,1)S(1)}, bf16[512,1,256]{0,2,1:T(8,128)(2,1)}, u32[]{:S(2)}) copy-start(bf16[512,1,256]{0,2,1:T(8,128)(2,1)} %get-tuple-element.24) | copy-start | bytes 786436
  189.0 8.7 %slice-start.9 = ((s8[10485760]{0:T(1024)(128)(4,1)}), s8[4194304]{0:T(1024)(128)(4,1)S(1)}, s32[]{:S(2)}) async-start(s8[10485760]{0:T(1024)(128)(4,1)} %bitcast.264), calls=%async_computation.10 | async-start | bytes 8388608
  189.0 8.7 %slice-start.10 = ((s8[10485760]{0:T(1024)(128)(4,1)}), s8[4194304]{0:T(1024)(128)(4,1)S(1)}, s32[]{:S(2)}) async-start(s8[10485760]{0:T(1024)(128)(4,1)} %bitcast.264), calls=%async_computation.11 | async-start | bytes 8388608
  192.7 5.0 %slice-start.11 = ((s8[10485760]{0:T(1024)(128)(4,1)}), s8[2097152]{0:T(1024)(128)(4,1)S(1)}, s32[]{:S(2)}) async-start(s8[10485760]{0:T(1024)(128)(4,1)} %bitcast.264), calls=%async_computation.12 | async-start | bytes 4194304
  192.7 7.2 %copy-start.4 = (bf16[512,1,256]{0,2,1:T(8,128)(2,1)S(1)}, bf16[512,1,256]{0,2,1:T(8,128)(2,1)}, u32[]{:S(2)}) copy-start(bf16[512,1,256]{0,2,1:T(8,128)(2,1)} %get-tuple-element.27) | copy-start | bytes 786436
  197.7 6.3 %slice-start.3 = ((s8[10485760]{0:T(1024)(128)(4,1)}), s8[4194304]{0:T(1024)(128)(4,1)S(1)}, s32[]{:S(2)}) async-start(s8[10485760]{0:T(1024)(128)(4,1)} %bitcast.260), calls=%async_computation.4 | async-start | bytes 8388608
  197.7 6.3 %slice-start.4 = ((s8[10485760]{0:T(1024)(128)(4,1)}), s8[4194304]{0:T(1024)(128)(4,1)S(1)}, s32[]{:S(2)}) async-start(s8[10485760]{0:T(1024)(128)(4,1)} %bitcast.260), calls=%async_computation.5 | async-start | bytes 8388608
  199.9 4.1 %slice-start.5 = ((s8[10485760]{0:T(1024)(128)(4,1)}), s8[2097152]{0:T(1024)(128)(4,1)S(1)}, s32[]{:S(2)}) async-start(s8[10485760]{0:T(1024)(128)(4,1)} %bitcast.260), calls=%async_computation.6 | async-start | bytes 4194304
  199.9 6.3 %copy-start.5 = (f32[2,5,512]{2,1,0:T(8,128)S(1)}, f32[2,5,512]{2,1,0:T(8,128)}, u32[]{:S(2)}) copy-start(f32[2,5,512]{2,1,0:T(8,128)} %fusion.4) | copy-start | bytes 61444
  199.9 6.4 %copy-start.1 = (bf16[512,1,256]{0,2,1:T(8,128)(2,1)S(1)}, bf16[512,1,256]{0,2,1:T(8,128)(2,1)}, u32[]{:S(2)}) copy-start(bf16[512,1,256]{0,2,1:T(8,128)(2,1)} %get-tuple-element.18) | copy-start | bytes 786436
  204.0 2.3 %copy-start.8 = (f32[2,5,512,128]{2,3,1,0:T(8,128)S(1)}, f32[2,5,512,128]{2,3,1,0:T(8,128)}, u32[]{:S(2)}) copy-start(f32[2,5,512,128]{2,3,1,0:T(8,128)} %fusion.23) | copy-start | bytes 7864324
  204.0 2.5 %copy-start.9 = (f32[2,5,512,128]{2,3,1,0:T(8,128)S(1)}, f32[2,5,512,128]{2,3,1,0:T(8,128)}, u32[]{:S(2)}) copy-start(f32[2,5,512,128]{2,3,1,0:T(8,128)} %fusion.21) | copy-start | bytes 7864324
  204.0 3.3 %copy-start.10 = (f32[2,5,512,128]{2,3,1,0:T(8,128)S(1)}, f32[2,5,512,128]{2,3,1,0:T(8,128)}, u32[]{:S(2)}) copy-start(f32[2,5,512,128]{2,3,1,0:T(8,128)} %fusion.19) | copy-start | bytes 7864324
